TPU v7x, 32 devices: a whole 2x2x4 slice. The times are simulated.
32 devices in a mesh: seq: 4 (over y, x), dp: 8 (over z, core).
Axes of the slice: x: 2, y: 2, z: 4, core: 2. Of those that a mesh axis runs over, the one named last changes fastest.
Arguments:
- tokens: bfloat16 [8, 2048, 768], P('dp', 'seq'), may hold values from -6 to 6
- doc_start: int32 [8, 2048], P('dp'), may hold values from 0 to 2047, as said below
- cotangent: bfloat16 [8, 2048, 768], P('dp', 'seq'), may hold values from -6 to 6
- norm_one: float32 [768], replicated, may hold values from 0.5 to 1.5
- w_qkv: bfloat16 [768, 2304], replicated, may hold values from -0.21875 to 0.21875
- w_out: bfloat16 [768, 768], replicated, may hold values from -0.875 to 0.875
- norm_two: float32 [768], replicated, may hold values from 0.5 to 1.5
- w_in: bfloat16 [768, 2304], replicated, may hold values from -0.21875 to 0.21875
- w_down: bfloat16 [1152, 768], replicated, may hold values from -0.1875 to 0.1875
Outputs:
- result: bfloat16 [8, 2048, 768], P('dp', 'seq')
- grad_tokens: float32 [8, 2048, 768], P('dp', 'seq')
- grad_norm_one: float32 [768], replicated
- grad_w_qkv: float32 [768, 2304], replicated
- grad_w_out: float32 [768, 768], replicated
- grad_norm_two: float32 [768], replicated
- grad_w_in: float32 [768, 2304], replicated
- grad_w_down: float32 [1152, 768], replicated
Inputs may be any that keep to these rules, and one draw needn't show every extreme that they name: Documents are contiguous: doc_start of a token is the place of the first token of its run of equal values, which begins at a place equal to that value; every row begins a document at 0 and ends with a document of one token at place 2048 - 1, and in every row one document starts before 2048 / 8 and runs to place 7 * 256 - 1 or further.
All inputs are finite; a program needn't handle non-finite values.
Results may differ from a plain program's by a relative error of at most 0.013.
Values may be sent and summed in bfloat16 or wider, within the bound.
No kernel may reach another device: no remote copies, remote signals or barrier semaphores. Data moves between devices by JAX's collectives and lax.ppermute only.
A program may use at most 128 MiB of HBM per device.

v0:
```python
import jax
import jax.numpy as jnp
from jax import lax
from jax.sharding import PartitionSpec as P

D = 768
HEADS = 12
HEAD_DIM = 64
FF = 1152
EPSILON = 1e-05
ROTARY_BASE = 160000.0
SCORE_SCALE = 0.125
MASKED_SCORE = -1e30


def layer_norm(values, gain_vec):
    average = jnp.mean(values, axis=-1, keepdims=True)
    centered = values - average
    variance = jnp.mean(centered * centered, axis=-1, keepdims=True)
    return centered * lax.rsqrt(variance + EPSILON) * gain_vec


def rotary_tables(offset):
    half_dim = HEAD_DIM // 2
    frequency = ROTARY_BASE ** (-(jnp.arange(half_dim, dtype=jnp.float32) * 2.0 / HEAD_DIM))
    angles = offset[:, None] * frequency[None, :]
    return (jnp.cos(angles)[:, None, :], jnp.sin(angles)[:, None, :])


def rotate(values, cosine, sine_table):
    half_dim = values.shape[-1] // 2
    first_half = values[..., :half_dim]
    second_half = values[..., half_dim:]
    return jnp.concatenate(
        [
            first_half * cosine - second_half * sine_table,
            second_half * cosine + first_half * sine_table,
        ],
        axis=-1,
    )


def unrotate_three(grad_wide, cosine, sine_table):
    negative_sine = -sine_table
    return jnp.stack(
        [
            rotate(grad_wide[:, 0], cosine, negative_sine),
            rotate(grad_wide[:, 1], cosine, negative_sine),
            grad_wide[:, 2],
        ],
        axis=1,
    )


def gelu_gate(gate_part, up_part):
    return jax.nn.gelu(gate_part, approximate=False) * up_part


def block_scores(query_block, key_heads, block_ids, starts):
    scores = (
        jnp.einsum("qhd,khd->hqk", query_block, key_heads, preferred_element_type=jnp.float32)
        * SCORE_SCALE
    )
    allowed = block_ids[:, None] == starts[None, :]
    return jnp.where(allowed[None], scores, MASKED_SCORE)


def attend_forward(queries, key_heads, value_heads, starts, block_rows):
    row_total = queries.shape[0]

    def attend_block(block_index):
        row_begin = block_index * block_rows
        query_block = lax.dynamic_slice_in_dim(queries, row_begin, block_rows)
        block_ids = lax.dynamic_slice_in_dim(starts, row_begin, block_rows)
        scores = block_scores(query_block, key_heads, block_ids, starts)
        row_max = jnp.max(scores, axis=-1, keepdims=True)
        weight = jnp.exp(scores - row_max)
        row_sum = jnp.sum(weight, axis=-1, keepdims=True)
        probs = (weight / row_sum).astype(jnp.bfloat16)
        context = jnp.einsum("hqk,khd->qhd", probs, value_heads, preferred_element_type=jnp.float32)
        return (context, row_max, row_sum)

    context, row_max, row_sum = lax.map(
        attend_block, jnp.arange(row_total // block_rows, dtype=jnp.int32)
    )
    return (context.reshape(queries.shape), row_max, row_sum)


def attend_backward(
    queries, key_heads, value_heads, grad_context, starts, row_max, row_sum, block_rows
):
    row_total = queries.shape[0]

    def back_block(carry, block_index):
        grad_key, grad_value = carry
        row_begin = block_index * block_rows
        query_block = lax.dynamic_slice_in_dim(queries, row_begin, block_rows)
        grad_block = lax.dynamic_slice_in_dim(grad_context, row_begin, block_rows)
        block_ids = lax.dynamic_slice_in_dim(starts, row_begin, block_rows)
        scores = block_scores(query_block, key_heads, block_ids, starts)
        probs = jnp.exp(scores - row_max[block_index]) / row_sum[block_index]
        probs_low = probs.astype(jnp.bfloat16)
        grad_value = grad_value + jnp.einsum(
            "hqk,qhd->khd", probs_low, grad_block, preferred_element_type=jnp.float32
        )
        grad_prob = jnp.einsum(
            "qhd,khd->hqk", grad_block, value_heads, preferred_element_type=jnp.float32
        )
        centre = jnp.sum(grad_prob * probs, axis=-1, keepdims=True)
        grad_scores = (probs * (grad_prob - centre)).astype(jnp.bfloat16)
        grad_query = (
            jnp.einsum("hqk,khd->qhd", grad_scores, key_heads, preferred_element_type=jnp.float32)
            * SCORE_SCALE
        )
        grad_key = (
            grad_key
            + jnp.einsum(
                "hqk,qhd->khd", grad_scores, query_block, preferred_element_type=jnp.float32
            )
            * SCORE_SCALE
        )
        return ((grad_key, grad_value), grad_query)

    zero_heads = jnp.zeros(queries.shape, jnp.float32)
    (grad_key, grad_value), grad_query = lax.scan(
        back_block, (zero_heads, zero_heads), jnp.arange(row_total // block_rows, dtype=jnp.int32)
    )
    return (grad_query.reshape(queries.shape), grad_key, grad_value)


def on_device(tokens, doc_start, cotangent, norm_one, w_qkv, w_out, norm_two, w_in, w_down):
    seq_parts = lax.axis_size("seq")
    shard_len = tokens.shape[1]
    row_total = shard_len * seq_parts
    head_width = D // seq_parts
    group_heads = HEADS // seq_parts
    block_rows = min(512, row_total)
    first_token = lax.axis_index("seq") * shard_len
    hidden = tokens[0].astype(jnp.float32)
    starts = doc_start[0]
    own_starts = lax.dynamic_slice_in_dim(starts, first_token, shard_len)
    offset = (first_token + jnp.arange(shard_len, dtype=jnp.int32) - own_starts).astype(jnp.float32)
    cosine, sine_table = rotary_tables(offset)
    normed_one, norm_one_back = jax.vjp(layer_norm, hidden, norm_one)
    normed_one_low = normed_one.astype(jnp.bfloat16)
    projected = jnp.dot(normed_one_low, w_qkv, preferred_element_type=jnp.float32).reshape(
        shard_len, 3, HEADS, HEAD_DIM
    )
    turned = jnp.stack(
        [
            rotate(projected[:, 0], cosine, sine_table),
            rotate(projected[:, 1], cosine, sine_table),
            projected[:, 2],
        ],
        axis=1,
    ).astype(jnp.bfloat16)
    outgoing = turned.reshape(shard_len, 3, seq_parts, head_width)
    incoming = lax.all_to_all(outgoing, "seq", split_axis=2, concat_axis=0, tiled=True)
    queries = incoming[:, 0, 0].reshape(row_total, group_heads, HEAD_DIM)
    key_heads = incoming[:, 1, 0].reshape(row_total, group_heads, HEAD_DIM)
    value_heads = incoming[:, 2, 0].reshape(row_total, group_heads, HEAD_DIM)
    context, row_max, row_sum = attend_forward(queries, key_heads, value_heads, starts, block_rows)
    context_send = context.astype(jnp.bfloat16).reshape(row_total, 1, head_width)
    context_tok = lax.all_to_all(
        context_send, "seq", split_axis=0, concat_axis=1, tiled=True
    ).reshape(shard_len, D)
    attended = jnp.dot(context_tok, w_out, preferred_element_type=jnp.float32)
    middle = hidden + attended
    normed_two, norm_two_back = jax.vjp(layer_norm, middle, norm_two)
    normed_two_low = normed_two.astype(jnp.bfloat16)
    gate_up = jnp.dot(normed_two_low, w_in, preferred_element_type=jnp.float32)
    inner, gelu_back = jax.vjp(gelu_gate, gate_up[:, :FF], gate_up[:, FF:])
    inner_low = inner.astype(jnp.bfloat16)
    result = (middle + jnp.dot(inner_low, w_down, preferred_element_type=jnp.float32)).astype(
        jnp.bfloat16
    )
    grad_out = cotangent[0]
    grad_w_down = jnp.einsum("tf,td->fd", inner_low, grad_out, preferred_element_type=jnp.float32)
    grad_inner = jnp.einsum("td,fd->tf", grad_out, w_down, preferred_element_type=jnp.float32)
    grad_gate, grad_up = gelu_back(grad_inner)
    grad_gate_up = jnp.concatenate([grad_gate, grad_up], axis=-1).astype(jnp.bfloat16)
    grad_w_in = jnp.einsum(
        "td,tf->df", normed_two_low, grad_gate_up, preferred_element_type=jnp.float32
    )
    grad_normed_two = jnp.einsum(
        "tf,df->td", grad_gate_up, w_in, preferred_element_type=jnp.float32
    )
    grad_middle_part, grad_norm_two = norm_two_back(grad_normed_two)
    grad_middle = grad_out.astype(jnp.float32) + grad_middle_part
    grad_mid_low = grad_middle.astype(jnp.bfloat16)
    grad_w_out = jnp.einsum(
        "td,te->de", context_tok, grad_mid_low, preferred_element_type=jnp.float32
    )
    grad_context_tok = jnp.einsum(
        "te,de->td", grad_mid_low, w_out, preferred_element_type=jnp.float32
    ).astype(jnp.bfloat16)
    grad_context = lax.all_to_all(
        grad_context_tok.reshape(shard_len, seq_parts, head_width),
        "seq",
        split_axis=1,
        concat_axis=0,
        tiled=True,
    )
    grad_context = grad_context.reshape(row_total, group_heads, HEAD_DIM)
    grad_query, grad_key, grad_value = attend_backward(
        queries, key_heads, value_heads, grad_context, starts, row_max, row_sum, block_rows
    )
    grad_heads = jnp.stack([grad_query, grad_key, grad_value], axis=1).astype(jnp.bfloat16)
    grad_tok = lax.all_to_all(
        grad_heads.reshape(row_total, 3, 1, head_width),
        "seq",
        split_axis=0,
        concat_axis=2,
        tiled=True,
    )
    grad_tok = grad_tok.reshape(shard_len, 3, HEADS, HEAD_DIM)
    grad_projected = unrotate_three(grad_tok.astype(jnp.float32), cosine, sine_table)
    grad_projected = grad_projected.astype(jnp.bfloat16).reshape(shard_len, 3 * D)
    grad_normed_one = jnp.einsum(
        "tf,df->td", grad_projected, w_qkv, preferred_element_type=jnp.float32
    )
    grad_hidden_part, grad_norm_one = norm_one_back(grad_normed_one)
    grad_input = grad_middle + grad_hidden_part
    grad_w_qkv = jnp.einsum(
        "td,tf->df", normed_one_low, grad_projected, preferred_element_type=jnp.float32
    )
    summed = lax.psum(
        (grad_norm_one, grad_w_qkv, grad_w_out, grad_norm_two, grad_w_in, grad_w_down),
        ("seq", "dp"),
    )
    return (
        result[None],
        grad_input[None],
        summed[0],
        summed[1],
        summed[2],
        summed[3],
        summed[4],
        summed[5],
    )


def solution(mesh):
    placed = (
        P("dp", "seq", None),
        P("dp", None),
        P("dp", "seq", None),
        P(),
        P(),
        P(),
        P(),
        P(),
        P(),
    )
    return jax.shard_map(
        on_device,
        mesh=mesh,
        in_specs=placed,
        out_specs=(P("dp", "seq", None), P("dp", "seq", None), P(), P(), P(), P(), P(), P()),
        check_vma=False,
    )
```

profile of v0, /device:TPU:0, one launch (start us, length us, event | category | flops | bytes accessed | tf_op | source)
XLA Modules:
  0.0 809.1 jit_solution(15965780885867940108)
XLA Ops:
  7.2 5.9 copy.68
  16.5 4.5 fusion.55
  30.1 5.4 all-to-all-start
  35.5 28.5 %all-to-all-done = bf16[512,3,4,192]{0,3,1,2:T(8,128)(2,1)} async-done(((bf16[512,3,4,192]{0,3,1,2:T(8,128)(2,1)}), bf16[512,3,4,192]{0,3,1,2:T(8,128)(2,1)}, u32[]{:S(2)}, u32[]{:S(2)}) %all-to-all-start) | async-done | bytes 2359328 | tf_op jit(solution)/shard_map/all_to_all | solution.py:158
  68.4 99.3 %while.29 = (s32[]{:T(128)}, bf16[4,512,3,64]{1,3,2,0:T(8,128)(2,1)}, f32[4,3,512,1]{2,1,3,0:T(4,128)}, f32[4,3,512,1]{2,1,3,0:T(4,128)}, s32[4]{0:T(128)S(1)}, ...) while((s32[]{:T(128)}, ...), condition=%wide.region_5.6_spmd, body=%wide.region_2.5_spmd.sunk | while | flops 844100608 | bytes 53621036 | solution.py:83
  70.4 8.3 %fusion.119 = (f32[3,512]{1,0:T(4,128)S(1)}, f32[3,512,2048]{2,1,0:T(8,128)}) fusion(pred[512,2048]{1,0:T(8,128)(4,1)S(1)} %broadcast_compare_fusion.4, bf16[2048,3,64]{0,2,1:T(8,128)(2,1)} %get-tuple-element.471, bf16[2048,3,64]{0,2,1:T(8,128)(2,1)} %get-tuple-element.470, s32[]{:T(128)S(6)} %select_n.52), kind=kOutput, calls=%fused_computation.3.clone.1 | convolution fusion | flops 412088832 | bytes 14620676 | tf_op jit(solution)/shard_map/while/body/eval_jaxpr/qhd,khd->hqk/dot_general | solution.py:61
  78.7 6.9 fusion.120
  85.6 6.8 fusion.121
  95.2 8.3 %fusion.119 = (f32[3,512]{1,0:T(4,128)S(1)}, f32[3,512,2048]{2,1,0:T(8,128)}) fusion(pred[512,2048]{1,0:T(8,128)(4,1)S(1)} %broadcast_compare_fusion.4, bf16[2048,3,64]{0,2,1:T(8,128)(2,1)} %get-tuple-element.471, bf16[2048,3,64]{0,2,1:T(8,128)(2,1)} %get-tuple-element.470, s32[]{:T(128)S(6)} %select_n.52), kind=kOutput, calls=%fused_computation.3.clone.1 | convolution fusion | flops 412088832 | bytes 14620676 | tf_op jit(solution)/shard_map/while/body/eval_jaxpr/qhd,khd->hqk/dot_general | solution.py:61
  103.5 6.9 fusion.120
  110.4 6.8 fusion.121
  120.0 8.3 %fusion.119 = (f32[3,512]{1,0:T(4,128)S(1)}, f32[3,512,2048]{2,1,0:T(8,128)}) fusion(pred[512,2048]{1,0:T(8,128)(4,1)S(1)} %broadcast_compare_fusion.4, bf16[2048,3,64]{0,2,1:T(8,128)(2,1)} %get-tuple-element.471, bf16[2048,3,64]{0,2,1:T(8,128)(2,1)} %get-tuple-element.470, s32[]{:T(128)S(6)} %select_n.52), kind=kOutput, calls=%fused_computation.3.clone.1 | convolution fusion | flops 412088832 | bytes 14620676 | tf_op jit(solution)/shard_map/while/body/eval_jaxpr/qhd,khd->hqk/dot_general | solution.py:61
  128.3 6.9 fusion.120
  135.2 6.8 fusion.121
  144.9 8.3 %fusion.119 = (f32[3,512]{1,0:T(4,128)S(1)}, f32[3,512,2048]{2,1,0:T(8,128)}) fusion(pred[512,2048]{1,0:T(8,128)(4,1)S(1)} %broadcast_compare_fusion.4, bf16[2048,3,64]{0,2,1:T(8,128)(2,1)} %get-tuple-element.471, bf16[2048,3,64]{0,2,1:T(8,128)(2,1)} %get-tuple-element.470, s32[]{:T(128)S(6)} %select_n.52), kind=kOutput, calls=%fused_computation.3.clone.1 | convolution fusion | flops 412088832 | bytes 14620676 | tf_op jit(solution)/shard_map/while/body/eval_jaxpr/qhd,khd->hqk/dot_general | solution.py:61
  153.2 6.9 fusion.120
  160.0 6.8 fusion.121
  170.3 2.8 convert_element_type.105
  173.6 3.0 reduce.1
  178.9 3.9 reshape.373
  182.8 15.3 %all_to_all.57 = bf16[4,2,49152]{2,1,0:T(2,128)(2,1)} all-to-all(bf16[4,2,49152]{2,1,0:T(2,128)(2,1)} %reshape.373), channel_id=1, replica_groups=mesh['seq'=4,'dp'=8] {'seq'}, dimensions={0} | all-to-all | bytes 1572864 | tf_op jit(solution)/shard_map/all_to_all | solution.py:164
  198.1 4.1 reshape.374
  202.2 5.7 copy.75
  208.0 3.4 all_to_all.47
  217.9 6.1 add_convert_fusion
  233.1 4.2 all-to-all-start.2
  237.3 9.3 %all-to-all-done.2 = bf16[512,4,192]{0,2,1:T(8,128)(2,1)} async-done(((bf16[512,4,192]{0,2,1:T(8,128)(2,1)}), bf16[512,4,192]{0,2,1:T(8,128)(2,1)}, u32[]{:S(2)}, u32[]{:S(2)}) %all-to-all-start.2) | async-done | bytes 786464 | tf_op jit(solution)/shard_map/all_to_all | solution.py:197
  249.2 2.8 reshape.369
  252.9 125.6 %while.30 = (s32[]{:T(128)}, f32[2048,3,64]{0,2,1:T(8,128)S(1)}, f32[2048,3,64]{0,2,1:T(8,128)S(1)}, bf16[4,512,3,64]{1,3,2,0:T(8,128)(2,1)}, s32[4]{0:T(128)S(1...) while((s32[]{:T(128)}, f32[2048,3,64]{0,2,1:T(8,128)S(1)}, ...), condition=%wide.region_12.13_spmd.clone, body=%wide.region_10.12_spmd.clone.sunk | while | flops 2047834624 | bytes 185006560 | solution.py:125
  257.6 5.0 exponential_divide_fusion.2
  262.6 4.1 multiply_reduce_fusion.5
  267.2 3.5 multiply_convert_fusion.7
  270.7 4.4 fusion.131
  275.1 6.2 fusion.132
  289.0 5.0 exponential_divide_fusion.2
  294.0 4.1 multiply_reduce_fusion.5
  298.5 3.5 multiply_convert_fusion.7
  302.0 4.4 fusion.131
  306.5 6.2 fusion.132
  320.3 5.0 exponential_divide_fusion.2
  325.3 4.1 multiply_reduce_fusion.5
  329.9 3.5 multiply_convert_fusion.7
  333.4 4.4 fusion.131
  337.8 6.2 fusion.132
  351.7 5.0 exponential_divide_fusion.2
  356.7 4.1 multiply_reduce_fusion.5
  361.3 3.5 multiply_convert_fusion.7
  364.7 4.4 fusion.131
  369.2 6.2 fusion.132
  383.4 4.7 copy.80
  388.1 5.0 all-to-all-start.3
  395.4 2.9 fusion.57
  398.4 5.1 fusion.51
  403.5 35.6 %all-to-all-done.3 = bf16[2048,3,1,192]{3,1,2,0:T(4,128)(2,1)} async-done(((bf16[2048,3,1,192]{3,1,2,0:T(4,128)(2,1)}), bf16[2048,3,1,192]{3,1,2,0:T(4,128)(2,1)}, u32[]{:S(2)}, u32[]{:S(2)}) %all-to-all-start.3) | async-done | bytes 2359328 | tf_op jit(solution)/shard_map/all_to_all | solution.py:209
  439.1 6.9 copy.81
  446.0 6.4 reshape.371
  452.5 3.9 copy.82
  459.7 5.3 fusion.61
  465.1 4.0 fusion.53
  473.3 40.5 %all-reduce = (f32[768]{0:T(1024)}, f32[768]{0:T(1024)}) all-reduce(f32[768]{0:T(1024)S(1)} %get-tuple-element.181, f32[768]{0:T(1024)S(1)} %copy-done.54), channel_id=1, replica_groups=mesh['seq'=4,'dp'=8] {'seq','dp'}, use_global_device_ids=true, to_apply=%region_16.17 | all-reduce | flops 1536 | bytes 12288 | tf_op jit(solution)/shard_map/psum | solution.py:227
  513.8 3.3 add_bitcast_fusion
  517.0 269.9 %all-reduce.4.cloned.1.call-done = (f32[768,2304]{1,0:T(8,128)}, f32[768,768]{1,0:T(8,128)}, f32[768,2304]{1,0:T(8,128)}, f32[1152,768]{1,0:T(8,128)}) async-done(((f32[768,2304]{1,0:T(8,128)}, f32[768,768]{1,0:T(8,128)}, f32[768,2304]{1,0:T(8,128)}, f32[1152,768]{1,0:T(8,128)}), (f32[768,2304]{1,0:T(8,128)}, f32[768,768]{1,0:T(8,128)}, f32[768,2304]{1,0:T(8,128)}, ...) | async-done | bytes 20054032 | tf_op jit(solution)/shard_map/psum | solution.py:227
  786.9 7.2 copy.118
  795.5 3.6 copy.120
  (273 shorter events, 90.1 us)
Async XLA Ops:
  7.2 208.6 %copy-start = (bf16[768,2304]{1,0:T(8,128)(2,1)S(1)}, bf16[768,2304]{1,0:T(8,128)(2,1)}, u32[]{:S(2)}) copy-start(bf16[768,2304]{1,0:T(8,128)(2,1)} %param.20) | copy-start | bytes 10616836
  7.2 9.3 %copy-start.52 = (f32[768]{0:T(1024)S(1)}, f32[768]{0:T(1024)}, u32[]{:S(2)}) copy-start(f32[768]{0:T(1024)} %param.16) | copy-start | bytes 9220
  14.4 6.5 copy-start.44
  16.5 4.5 copy-start.46
  24.9 2.4 copy-start.35
  30.1 34.0 %all-to-all-start = ((bf16[512,3,4,192]{0,3,1,2:T(8,128)(2,1)}), bf16[512,3,4,192]{0,3,1,2:T(8,128)(2,1)}, u32[]{:S(2)}, u32[]{:S(2)}) async-start(bf16[512,3,4,192]{0,3,1,2:T(8,128)(2,1)} %pad_maximum_fusion), calls=%async_computation | async-start | bytes 4718592 | tf_op jit(solution)/shard_map/all_to_all | solution.py:158
  78.7 6.9 copy-start.3
  78.7 6.9 copy-start.23
  103.5 6.9 copy-start.3
  103.5 6.9 copy-start.23
  128.3 6.9 copy-start.3
  128.3 6.9 copy-start.23
  153.1 6.9 copy-start.3
  153.2 6.9 copy-start.23
  212.7 3.0 copy-start.25
  212.7 3.1 copy-start.38
  215.4 13.2 %copy-start.5 = (f32[512,768]{1,0:T(8,128)}, f32[512,768]{1,0:T(8,128)S(1)}, u32[]{:S(2)}) copy-start(f32[512,768]{1,0:T(8,128)S(1)} %get-tuple-element.272) | copy-start | bytes 4718596
  215.4 13.2 %copy-start.40 = (f32[512]{0:T(512)}, f32[512]{0:T(512)S(1)}, u32[]{:S(2)}) copy-start(f32[512]{0:T(512)S(1)} %broadcast_multiply_fusion) | copy-start | bytes 6148
  215.7 12.8 %copy-start.42 = (f32[512]{0:T(512)}, f32[512]{0:T(512)S(1)}, u32[]{:S(2)}) copy-start(f32[512]{0:T(512)S(1)} %fusion.65) | copy-start | bytes 6148
  215.8 2.1 copy-start.11
  225.7 2.8 copy-start.15
  229.2 2.7 copy-start.7
  233.1 13.5 %all-to-all-start.2 = ((bf16[512,4,192]{0,2,1:T(8,128)(2,1)}), bf16[512,4,192]{0,2,1:T(8,128)(2,1)}, u32[]{:S(2)}, u32[]{:S(2)}) async-start(bf16[512,4,192]{0,2,1:T(8,128)(2,1)} %bitcast.31), calls=%async_computation.2 | async-start | bytes 1572864 | tf_op jit(solution)/shard_map/all_to_all | solution.py:197
  262.6 4.6 copy-start.2
  270.7 10.7 %slice-start = ((s8[6291456]{0:T(1024)(128)(4,1)}), s8[4194304]{0:T(1024)(128)(4,1)S(1)}, s32[]{:S(2)}) async-start(s8[6291456]{0:T(1024)(128)(4,1)} %bitcast.196), calls=%async_computation.5 | async-start | bytes 8388608 | tf_op jit(solution)/shard_map/while
  275.1 6.3 slice-start.1
  275.1 6.3 copy-start.4
  275.1 6.3 copy-start.20
  294.0 4.6 copy-start.2
  302.0 10.7 %slice-start = ((s8[6291456]{0:T(1024)(128)(4,1)}), s8[4194304]{0:T(1024)(128)(4,1)S(1)}, s32[]{:S(2)}) async-start(s8[6291456]{0:T(1024)(128)(4,1)} %bitcast.196), calls=%async_computation.5 | async-start | bytes 8388608 | tf_op jit(solution)/shard_map/while
  306.4 6.3 slice-start.1
  306.4 6.3 copy-start.4
  306.5 6.3 copy-start.20
  325.3 4.6 copy-start.2
  333.4 10.7 %slice-start = ((s8[6291456]{0:T(1024)(128)(4,1)}), s8[4194304]{0:T(1024)(128)(4,1)S(1)}, s32[]{:S(2)}) async-start(s8[6291456]{0:T(1024)(128)(4,1)} %bitcast.196), calls=%async_computation.5 | async-start | bytes 8388608 | tf_op jit(solution)/shard_map/while
  337.8 6.3 slice-start.1
  337.8 6.3 copy-start.4
  337.8 6.3 copy-start.20
  356.7 4.6 copy-start.2
  364.7 10.7 %slice-start = ((s8[6291456]{0:T(1024)(128)(4,1)}), s8[4194304]{0:T(1024)(128)(4,1)S(1)}, s32[]{:S(2)}) async-start(s8[6291456]{0:T(1024)(128)(4,1)} %bitcast.196), calls=%async_computation.5 | async-start | bytes 8388608 | tf_op jit(solution)/shard_map/while
  369.2 6.3 slice-start.1
  369.2 6.3 copy-start.4
  369.2 6.3 copy-start.20
  388.1 5.1 copy-start.26
  388.1 5.1 copy-start.28
  388.1 51.0 %all-to-all-start.3 = ((bf16[2048,3,1,192]{3,1,2,0:T(4,128)(2,1)}), bf16[2048,3,1,192]{3,1,2,0:T(4,128)(2,1)}, u32[]{:S(2)}, u32[]{:S(2)}) async-start(bf16[2048,3,1,192]{3,1,2,0:T(4,128)(2,1)} %copy.80), calls=%async_computation.3 | async-start | bytes 8388608 | tf_op jit(solution)/shard_map/all_to_all | solution.py:209
  393.1 2.2 copy-start.12
  393.1 393.7 %all-reduce.4.cloned.1.call-start = ((), (), s32[]{:S(2)}) async-start(), calls=%async_computation.4 | async-start | bytes 40108032 | tf_op jit(solution)/shard_map/psum | solution.py:227
  393.2 2.2 copy-start.13
  395.4 3.0 copy-start.6
  395.4 3.0 copy-start.16
  395.4 3.0 copy-start.34
  395.4 3.0 copy-start.39
  395.4 2.9 copy-start.41
  395.4 2.9 copy-start.43
  465.0 4.1 copy-start.17
  465.0 4.1 copy-start.31
  469.1 2.3 copy-start.51
  471.4 42.4 %copy-start.8 = (f32[512,768]{1,0:T(8,128)S(1)}, f32[512,768]{1,0:T(8,128)}, u32[]{:S(2)}) copy-start(f32[512,768]{1,0:T(8,128)} %copy-done.7) | copy-start | bytes 4718596
  471.4 42.4 %copy-start.49 = (f32[512]{0:T(512)S(1)}, f32[512]{0:T(512)}, u32[]{:S(2)}) copy-start(f32[512]{0:T(512)} %copy-done.48) | copy-start | bytes 6148
  786.9 7.2 copy-start.29
  786.9 8.6 %copy-start.10 = (f32[768,2304]{1,0:T(8,128)S(1)}, f32[768,2304]{1,0:T(8,128)}, u32[]{:S(2)}) copy-start(f32[768,2304]{1,0:T(8,128)} %get-tuple-element.537) | copy-start | bytes 21233668
  795.5 4.6 copy-start.18
  795.5 6.4 copy-start.1
  (26 other events, 34.0 us)
Sparse Core Ops, SparseCore 0:
  465.2 321.6 all-reduce.3
where the time goes:
time: 816 us; the launch traced here: 809 us
  waiting for transfers between devices  343 us (42%)
  matrix products  188 us (23%)
  local copies, waits for them, and re-layouts  109 us (13%)
  other arithmetic  69.3 us (8%)
  blocking collectives  55.8 us (7%)
  between operations  15.1 us (2%)
  starting transfers between devices  14.6 us (2%)
  loops' own time  13.8 us (2%)
    psum x1, waiting for transfers between devices, on_device(): lax.psum((grad_norm_one, grad_w_qkv, grad_w_out, grad_norm_two, grad_w_in...  270 us
    dot_general x8, matrix products, block_scores(): jnp.einsum('qhd,khd->hqk', query_block, key_heads, preferred_element_type...  53.2 us
    psum x1, blocking collectives, on_device(): lax.psum((grad_norm_one, grad_w_qkv, grad_w_out, grad_norm_two, grad_w_in...  40.5 us
    unnamed x108, local copies, waits for them, and re-layouts  37.3 us
    all_to_all x1, waiting for transfers between devices, on_device(): lax.all_to_all(grad_heads.reshape(row_total, 3, 1, head_width), 'seq', sp...  35.6 us
    all_to_all x1, waiting for transfers between devices, on_device(): lax.all_to_all(outgoing, 'seq', split_axis=2, concat_axis=0, tiled=True)  28.5 us
    reduce_sum x4, other arithmetic, attend_block(): row_sum = jnp.sum(weight, axis=-1, keepdims=True)  27.5 us
    dot_general x4, matrix products, attend_block(): jnp.einsum('hqk,khd->qhd', probs, value_heads, preferred_element_type=jnp...  27 us
  transfers between devices with their start and end apart: 4, of which 4 were waited for; matrix products, arithmetic and copies ran while one was open for 3% of the time, Pallas kernels for 0%

commit v1 on v0

--- a/solution.py
+++ b/solution.py
@@ -11,6 +11,29 @@
 ROTARY_BASE = 160000.0
 SCORE_SCALE = 0.125
 MASKED_SCORE = -1e30
+
+
+def cut_along(x, dim, size):
+    shape = x.shape
+    pieces = x.reshape(*shape[:dim], size, shape[dim] // size, *shape[dim + 1 :])
+    return jnp.moveaxis(pieces, dim, 0)
+
+
+def joined_along(tiles, dim):
+    tiles = jnp.moveaxis(tiles, 0, dim)
+    shape = tiles.shape
+    return tiles.reshape(*shape[:dim], shape[dim] * shape[dim + 1], *shape[dim + 2 :])
+
+
+def swapped_with_each(value, axis, split_dim, concat_dim):
+    size, index = (lax.axis_size(axis), lax.axis_index(axis))
+    tiles = cut_along(value, split_dim, size)
+    done = [tiles[index]]
+    for hop in range(1, size):
+        sent = tiles[index ^ hop]
+        done.append(lax.ppermute(sent, axis, [(i, i ^ hop) for i in range(size)]))
+    tiles = jnp.stack(done)[index ^ jnp.arange(size)]
+    return joined_along(tiles, concat_dim)
 
 
 def layer_norm(values, gain_vec):
@@ -206,13 +229,7 @@
         queries, key_heads, value_heads, grad_context, starts, row_max, row_sum, block_rows
     )
     grad_heads = jnp.stack([grad_query, grad_key, grad_value], axis=1).astype(jnp.bfloat16)
-    grad_tok = lax.all_to_all(
-        grad_heads.reshape(row_total, 3, 1, head_width),
-        "seq",
-        split_axis=0,
-        concat_axis=2,
-        tiled=True,
-    )
+    grad_tok = swapped_with_each(grad_heads.reshape(row_total, 3, 1, head_width), "seq", 0, 2)
     grad_tok = grad_tok.reshape(shard_len, 3, HEADS, HEAD_DIM)
     grad_projected = unrotate_three(grad_tok.astype(jnp.float32), cosine, sine_table)
     grad_projected = grad_projected.astype(jnp.bfloat16).reshape(shard_len, 3 * D)

time: 816 us -> 775 us (0.950)
  waiting for transfers between devices: 343 us -> 316 us
  local copies, waits for them, and re-layouts: 109 us -> 94.5 us
    all_to_all x1 -> x0, waiting for transfers between devices: 35.6 us -> none  [on_device(): lax.all_to_all(grad_heads.reshape(row_total, 3, 1, head_width), 'seq', sp...]
    ppermute x0 -> x3, waiting for transfers between devices: none -> 15.3 us  [swapped_with_each(): done.append(lax.ppermute(sent, axis, [(i, i ^ hop) for i in range(size)]))]
    convert_element_type x2 -> x1, local copies, waits for them, and re-layouts: 10.3 us -> 0.51 us  [on_device(): grad_tok.astype(jnp.float32)]
  transfers between devices with their start and end apart: 4 -> 6, of which waited for: 4 -> 5; matrix products, arithmetic and copies ran while one was open for 3% -> 3% of each run, Pallas kernels for 0% -> 0%
where the time goes in v1:
time: 775 us; the launch traced here: 769 us
  waiting for transfers between devices  316 us (41%)
  matrix products  190 us (25%)
  local copies, waits for them, and re-layouts  94.5 us (12%)
  other arithmetic  70.9 us (9%)
  blocking collectives  56.1 us (7%)
  between operations  15.1 us (2%)
  loops' own time  13.6 us (2%)
  starting transfers between devices  13.1 us (2%)
    psum x1, waiting for transfers between devices, on_device(): lax.psum((grad_norm_one, grad_w_qkv, grad_w_out, grad_norm_two, grad_w_in...  268 us
    dot_general x8, matrix products, block_scores(): jnp.einsum('qhd,khd->hqk', query_block, key_heads, preferred_element_type...  53.2 us
    psum x1, blocking collectives, on_device(): lax.psum((grad_norm_one, grad_w_qkv, grad_w_out, grad_norm_two, grad_w_in...  40.7 us
    unnamed x108, local copies, waits for them, and re-layouts  39 us
    all_to_all x1, waiting for transfers between devices, on_device(): lax.all_to_all(outgoing, 'seq', split_axis=2, concat_axis=0, tiled=True)  28.5 us
    reduce_sum x4, other arithmetic, attend_block(): row_sum = jnp.sum(weight, axis=-1, keepdims=True)  27.5 us
    dot_general x4, matrix products, attend_block(): jnp.einsum('hqk,khd->qhd', probs, value_heads, preferred_element_type=jnp...  27 us
    dot_general x4, matrix products, back_block(): jnp.einsum('hqk,qhd->khd', probs_low, grad_block, preferred_element_type=...  24.9 us
  transfers between devices with their start and end apart: 6, of which 5 were waited for; matrix products, arithmetic and copies ran while one was open for 3% of the time, Pallas kernels for 0%

profile of v1, /device:TPU:0, one launch (start us, length us, event | category | flops | bytes accessed | tf_op | source)
XLA Modules:
  0.0 769.0 jit_solution(16149336112347676856)
XLA Ops:
  7.2 5.9 copy.40
  16.5 4.5 fusion.55
  30.1 5.4 all-to-all-start
  35.5 28.5 %all-to-all-done = bf16[512,3,4,192]{0,3,1,2:T(8,128)(2,1)} async-done(((bf16[512,3,4,192]{0,3,1,2:T(8,128)(2,1)}), bf16[512,3,4,192]{0,3,1,2:T(8,128)(2,1)}, u32[]{:S(2)}, u32[]{:S(2)}) %all-to-all-start) | async-done | bytes 2359328 | tf_op jit(solution)/shard_map/all_to_all | solution.py:181
  68.4 99.3 %while.29 = (s32[]{:T(128)}, bf16[4,512,3,64]{1,3,2,0:T(8,128)(2,1)}, f32[4,3,512,1]{2,1,3,0:T(4,128)}, f32[4,3,512,1]{2,1,3,0:T(4,128)}, s32[4]{0:T(128)S(1)}, ...) while((s32[]{:T(128)}, ...), condition=%wide.region_5.6_spmd, body=%wide.region_2.5_spmd.sunk | while | flops 844100608 | bytes 53621036 | solution.py:106
  70.4 8.3 %fusion.120 = (f32[3,512]{1,0:T(4,128)S(1)}, f32[3,512,2048]{2,1,0:T(8,128)}) fusion(pred[512,2048]{1,0:T(8,128)(4,1)S(1)} %broadcast_compare_fusion.4, bf16[2048,3,64]{0,2,1:T(8,128)(2,1)} %get-tuple-element.475, bf16[2048,3,64]{0,2,1:T(8,128)(2,1)} %get-tuple-element.474, s32[]{:T(128)S(6)} %select_n.82), kind=kOutput, calls=%fused_computation.4.clone.1 | convolution fusion | flops 412088832 | bytes 14620676 | tf_op jit(solution)/shard_map/while/body/eval_jaxpr/qhd,khd->hqk/dot_general | solution.py:84
  78.7 6.9 fusion.121
  85.6 6.8 fusion.122
  95.2 8.3 %fusion.120 = (f32[3,512]{1,0:T(4,128)S(1)}, f32[3,512,2048]{2,1,0:T(8,128)}) fusion(pred[512,2048]{1,0:T(8,128)(4,1)S(1)} %broadcast_compare_fusion.4, bf16[2048,3,64]{0,2,1:T(8,128)(2,1)} %get-tuple-element.475, bf16[2048,3,64]{0,2,1:T(8,128)(2,1)} %get-tuple-element.474, s32[]{:T(128)S(6)} %select_n.82), kind=kOutput, calls=%fused_computation.4.clone.1 | convolution fusion | flops 412088832 | bytes 14620676 | tf_op jit(solution)/shard_map/while/body/eval_jaxpr/qhd,khd->hqk/dot_general | solution.py:84
  103.5 6.9 fusion.121
  110.4 6.8 fusion.122
  120.0 8.3 %fusion.120 = (f32[3,512]{1,0:T(4,128)S(1)}, f32[3,512,2048]{2,1,0:T(8,128)}) fusion(pred[512,2048]{1,0:T(8,128)(4,1)S(1)} %broadcast_compare_fusion.4, bf16[2048,3,64]{0,2,1:T(8,128)(2,1)} %get-tuple-element.475, bf16[2048,3,64]{0,2,1:T(8,128)(2,1)} %get-tuple-element.474, s32[]{:T(128)S(6)} %select_n.82), kind=kOutput, calls=%fused_computation.4.clone.1 | convolution fusion | flops 412088832 | bytes 14620676 | tf_op jit(solution)/shard_map/while/body/eval_jaxpr/qhd,khd->hqk/dot_general | solution.py:84
  128.3 6.9 fusion.121
  135.2 6.8 fusion.122
  144.9 8.3 %fusion.120 = (f32[3,512]{1,0:T(4,128)S(1)}, f32[3,512,2048]{2,1,0:T(8,128)}) fusion(pred[512,2048]{1,0:T(8,128)(4,1)S(1)} %broadcast_compare_fusion.4, bf16[2048,3,64]{0,2,1:T(8,128)(2,1)} %get-tuple-element.475, bf16[2048,3,64]{0,2,1:T(8,128)(2,1)} %get-tuple-element.474, s32[]{:T(128)S(6)} %select_n.82), kind=kOutput, calls=%fused_computation.4.clone.1 | convolution fusion | flops 412088832 | bytes 14620676 | tf_op jit(solution)/shard_map/while/body/eval_jaxpr/qhd,khd->hqk/dot_general | solution.py:84
  153.2 6.9 fusion.121
  160.1 6.8 fusion.122
  167.7 2.6 copy.45
  170.3 2.8 convert_element_type.102
  173.6 3.0 reduce.1
  178.9 3.9 reshape.394
  182.8 15.3 %all_to_all.48 = bf16[4,2,49152]{2,1,0:T(2,128)(2,1)} all-to-all(bf16[4,2,49152]{2,1,0:T(2,128)(2,1)} %reshape.394), channel_id=1, replica_groups=mesh['seq'=4,'dp'=8] {'seq'}, dimensions={0} | all-to-all | bytes 1572864 | tf_op jit(solution)/shard_map/all_to_all | solution.py:187
  198.1 4.1 reshape.395
  202.2 5.7 copy.47
  208.0 3.4 all_to_all.40
  212.6 2.7 fusion.76
  217.8 6.1 add_convert_fusion
  225.7 2.8 multiply_reduce_fusion.1
  233.0 4.2 all-to-all-start.2
  237.9 4.4 fusion.57
  242.3 4.3 all-to-all-done.2
  246.5 2.6 copy.50
  249.2 3.0 reshape.380
  253.1 125.4 %while.30 = (s32[]{:T(128)}, f32[2048,3,64]{0,2,1:T(8,128)S(1)}, f32[2048,3,64]{0,2,1:T(8,128)S(1)}, bf16[4,512,3,64]{1,3,2,0:T(8,128)(2,1)}, s32[4]{0:T(128)S(1...) while((s32[]{:T(128)}, f32[2048,3,64]{0,2,1:T(8,128)S(1)}, ...), condition=%wide.region_12.13_spmd.clone, body=%wide.region_10.12_spmd.clone.sunk | while | flops 2047834624 | bytes 185006560 | solution.py:148
  257.7 5.0 exponential_divide_fusion.2
  262.8 4.1 multiply_reduce_fusion.5
  267.3 3.5 multiply_convert_fusion.7
  270.8 4.4 fusion.132
  275.2 6.2 fusion.133
  289.1 5.0 exponential_divide_fusion.2
  294.1 4.1 multiply_reduce_fusion.5
  298.7 3.5 multiply_convert_fusion.7
  302.2 4.4 fusion.132
  306.6 6.2 fusion.133
  320.5 5.0 exponential_divide_fusion.2
  325.5 4.1 multiply_reduce_fusion.5
  330.0 3.5 multiply_convert_fusion.7
  333.5 4.4 fusion.132
  338.0 6.2 fusion.133
  351.8 5.0 exponential_divide_fusion.2
  356.8 4.1 multiply_reduce_fusion.5
  361.4 3.5 multiply_convert_fusion.7
  364.9 4.4 fusion.132
  369.3 6.2 fusion.133
  390.6 5.1 fusion.51
  395.7 6.3 collective-permute-done.2
  402.0 8.9 %collective-permute-done.1 = bf16[512,3,1,192]{0,3,1,2:T(8,128)(2,1)S(1)} collective-permute-done((bf16[512,3,1,192]{0,3,1,2:T(8,128)(2,1)S(1)}, bf16[512,3,1,192]{0,3,1,2:T(8,128)(2,1)S(1)}, u32[]{:S(2)}, u32[]{:S(2)}) %collective-permute-start.1) | collective-permute-done | bytes 589856 | tf_op jit(solution)/shard_map/ppermute | solution.py:34
  419.7 5.3 fusion.61
  426.7 3.7 fusion.53
  434.9 40.7 %all-reduce = (f32[768]{0:T(1024)}, f32[768]{0:T(1024)}) all-reduce(f32[768]{0:T(1024)S(1)} %get-tuple-element.181, f32[768]{0:T(1024)S(1)} %copy-done.54), channel_id=1, replica_groups=mesh['seq'=4,'dp'=8] {'seq','dp'}, use_global_device_ids=true, to_apply=%region_16.17 | all-reduce | flops 1536 | bytes 12288 | tf_op jit(solution)/shard_map/psum | solution.py:244
  475.6 3.2 add_bitcast_fusion
  478.9 268.0 %all-reduce.4.cloned.1.call-done = (f32[768,2304]{1,0:T(8,128)}, f32[768,768]{1,0:T(8,128)}, f32[768,2304]{1,0:T(8,128)}, f32[1152,768]{1,0:T(8,128)}) async-done(((f32[768,2304]{1,0:T(8,128)}, f32[768,768]{1,0:T(8,128)}, f32[768,2304]{1,0:T(8,128)}, f32[1152,768]{1,0:T(8,128)}), (f32[768,2304]{1,0:T(8,128)}, f32[768,768]{1,0:T(8,128)}, f32[768,2304]{1,0:T(8,128)}, ...) | async-done | bytes 20054032 | tf_op jit(solution)/shard_map/psum | solution.py:244
  746.9 7.2 copy.89
  755.5 3.6 copy.91
  (282 shorter events, 92.2 us)
Async XLA Ops:
  7.2 208.5 %copy-start = (bf16[768,2304]{1,0:T(8,128)(2,1)S(1)}, bf16[768,2304]{1,0:T(8,128)(2,1)}, u32[]{:S(2)}) copy-start(bf16[768,2304]{1,0:T(8,128)(2,1)} %param.20) | copy-start | bytes 10616836
  7.2 9.3 %copy-start.52 = (f32[768]{0:T(1024)S(1)}, f32[768]{0:T(1024)}, u32[]{:S(2)}) copy-start(f32[768]{0:T(1024)} %param.16) | copy-start | bytes 9220
  14.4 6.5 copy-start.44
  16.5 4.5 copy-start.46
  24.9 2.4 copy-start.35
  30.1 33.9 %all-to-all-start = ((bf16[512,3,4,192]{0,3,1,2:T(8,128)(2,1)}), bf16[512,3,4,192]{0,3,1,2:T(8,128)(2,1)}, u32[]{:S(2)}, u32[]{:S(2)}) async-start(bf16[512,3,4,192]{0,3,1,2:T(8,128)(2,1)} %pad_maximum_fusion), calls=%async_computation | async-start | bytes 4718592 | tf_op jit(solution)/shard_map/all_to_all | solution.py:181
  78.7 6.9 copy-start.3
  78.7 6.9 copy-start.23
  103.5 6.9 copy-start.3
  103.5 6.9 copy-start.23
  128.3 6.9 copy-start.3
  128.3 6.9 copy-start.23
  153.2 6.9 copy-start.3
  153.2 6.9 copy-start.23
  212.6 3.0 copy-start.25
  212.6 3.1 copy-start.38
  215.3 13.2 %copy-start.5 = (f32[512,768]{1,0:T(8,128)}, f32[512,768]{1,0:T(8,128)S(1)}, u32[]{:S(2)}) copy-start(f32[512,768]{1,0:T(8,128)S(1)} %get-tuple-element.276) | copy-start | bytes 4718596
  215.3 13.2 %copy-start.40 = (f32[512]{0:T(512)}, f32[512]{0:T(512)S(1)}, u32[]{:S(2)}) copy-start(f32[512]{0:T(512)S(1)} %broadcast_multiply_fusion) | copy-start | bytes 6148
  215.7 12.8 %copy-start.42 = (f32[512]{0:T(512)}, f32[512]{0:T(512)S(1)}, u32[]{:S(2)}) copy-start(f32[512]{0:T(512)S(1)} %fusion.65) | copy-start | bytes 6148
  225.7 2.8 copy-start.16
  229.2 2.7 copy-start.8
  233.0 13.5 %all-to-all-start.2 = ((bf16[512,4,192]{0,2,1:T(8,128)(2,1)}), bf16[512,4,192]{0,2,1:T(8,128)(2,1)}, u32[]{:S(2)}, u32[]{:S(2)}) async-start(bf16[512,4,192]{0,2,1:T(8,128)(2,1)} %bitcast.31), calls=%async_computation.2 | async-start | bytes 1572864 | tf_op jit(solution)/shard_map/all_to_all | solution.py:220
  237.2 509.7 %all-reduce.4.cloned.1.call-start = ((), (), s32[]{:S(2)}) async-start(), calls=%async_computation.3 | async-start | bytes 40108032 | tf_op jit(solution)/shard_map/psum | solution.py:244
  262.8 4.6 copy-start.2
  270.8 10.7 %slice-start = ((s8[6291456]{0:T(1024)(128)(4,1)}), s8[4194304]{0:T(1024)(128)(4,1)S(1)}, s32[]{:S(2)}) async-start(s8[6291456]{0:T(1024)(128)(4,1)} %bitcast.210), calls=%async_computation.4 | async-start | bytes 8388608 | tf_op jit(solution)/shard_map/while
  275.2 6.3 slice-start.1
  275.2 6.3 copy-start.4
  275.2 6.3 copy-start.21
  294.1 4.6 copy-start.2
  302.2 10.7 %slice-start = ((s8[6291456]{0:T(1024)(128)(4,1)}), s8[4194304]{0:T(1024)(128)(4,1)S(1)}, s32[]{:S(2)}) async-start(s8[6291456]{0:T(1024)(128)(4,1)} %bitcast.210), calls=%async_computation.4 | async-start | bytes 8388608 | tf_op jit(solution)/shard_map/while
  306.6 6.3 slice-start.1
  306.6 6.3 copy-start.4
  306.6 6.3 copy-start.21
  325.5 4.6 copy-start.2
  333.5 10.7 %slice-start = ((s8[6291456]{0:T(1024)(128)(4,1)}), s8[4194304]{0:T(1024)(128)(4,1)S(1)}, s32[]{:S(2)}) async-start(s8[6291456]{0:T(1024)(128)(4,1)} %bitcast.210), calls=%async_computation.4 | async-start | bytes 8388608 | tf_op jit(solution)/shard_map/while
  337.9 6.3 slice-start.1
  337.9 6.3 copy-start.4
  338.0 6.3 copy-start.21
  356.8 4.6 copy-start.2
  364.9 10.7 %slice-start = ((s8[6291456]{0:T(1024)(128)(4,1)}), s8[4194304]{0:T(1024)(128)(4,1)S(1)}, s32[]{:S(2)}) async-start(s8[6291456]{0:T(1024)(128)(4,1)} %bitcast.210), calls=%async_computation.4 | async-start | bytes 8388608 | tf_op jit(solution)/shard_map/while
  369.3 6.3 slice-start.1
  369.3 6.3 copy-start.4
  369.3 6.3 copy-start.21
  384.4 3.9 copy-start.26
  384.4 3.9 copy-start.28
  384.4 6.1 copy-start.41
  384.4 6.1 copy-start.43
  384.8 5.8 copy-start.6
  384.8 5.8 copy-start.17
  384.8 5.8 copy-start.34
  384.8 5.8 copy-start.39
  384.8 17.2 %collective-permute-start.2 = (bf16[512,3,1,192]{0,3,1,2:T(8,128)(2,1)S(1)}, bf16[512,3,1,192]{0,3,1,2:T(8,128)(2,1)S(1)}, u32[]{:S(2)}, u32[]{:S(2)}) collective-permute-start(bf16[512,3,1,192]{0,3,1,2:T(8,128)(2,1)S(1)} %get-tuple-element.254), channel_id=1, source_target_pairs={{0,24},{8,16},{16,8},{24,0},{1,25},{9,17},{17,9},{25,1},{2,26},{10... | collective-permute-start | bytes 1769480 | tf_op jit(solution)/shard_map/ppermute | solution.py:34
  386.3 24.7 %collective-permute-start.1 = (bf16[512,3,1,192]{0,3,1,2:T(8,128)(2,1)S(1)}, bf16[512,3,1,192]{0,3,1,2:T(8,128)(2,1)S(1)}, u32[]{:S(2)}, u32[]{:S(2)}) collective-permute-start(bf16[512,3,1,192]{0,3,1,2:T(8,128)(2,1)S(1)} %get-tuple-element.255), channel_id=1, source_target_pairs={{0,16},{8,24},{16,0},{24,8},{1,17},{9,25},{17,1},{25,9},{2,18},{10... | collective-permute-start | bytes 1769480 | tf_op jit(solution)/shard_map/ppermute | solution.py:34
  387.7 23.2 %collective-permute-start = (bf16[512,3,1,192]{0,3,1,2:T(8,128)(2,1)S(1)}, bf16[512,3,1,192]{0,3,1,2:T(8,128)(2,1)S(1)}, u32[]{:S(2)}, u32[]{:S(2)}) collective-permute-start(bf16[512,3,1,192]{0,3,1,2:T(8,128)(2,1)S(1)} %get-tuple-element.256), channel_id=1, source_target_pairs={{0,8},{8,0},{16,24},{24,16},{1,9},{9,1},{17,25},{25,17},{2,10},{10... | collective-permute-start | bytes 1769480 | tf_op jit(solution)/shard_map/ppermute | solution.py:34
  426.7 3.7 copy-start.18
  426.7 3.7 copy-start.31
  430.4 2.6 copy-start.51
  433.0 42.7 %copy-start.9 = (f32[512,768]{1,0:T(8,128)S(1)}, f32[512,768]{1,0:T(8,128)}, u32[]{:S(2)}) copy-start(f32[512,768]{1,0:T(8,128)} %copy-done.8) | copy-start | bytes 4718596
  433.0 42.6 %copy-start.13 = (bf16[1,512,768]{2,1,0:T(8,128)(2,1)S(1)}, bf16[1,512,768]{2,1,0:T(8,128)(2,1)}, u32[]{:S(2)}) copy-start(bf16[1,512,768]{2,1,0:T(8,128)(2,1)} %param.15) | copy-start | bytes 2359300
  433.0 42.6 %copy-start.49 = (f32[512]{0:T(512)S(1)}, f32[512]{0:T(512)}, u32[]{:S(2)}) copy-start(f32[512]{0:T(512)} %copy-done.48) | copy-start | bytes 6148
  746.9 7.2 copy-start.29
  746.9 8.6 %copy-start.11 = (f32[768,2304]{1,0:T(8,128)S(1)}, f32[768,2304]{1,0:T(8,128)}, u32[]{:S(2)}) copy-start(f32[768,2304]{1,0:T(8,128)} %get-tuple-element.541) | copy-start | bytes 21233668
  755.5 4.6 copy-start.19
  755.5 6.4 copy-start.1
  (28 other events, 37.3 us)
Sparse Core Ops, SparseCore 0:
  425.1 321.7 all-reduce.3
